TPU v7x, 256 devices: a whole 4x4x8 slice. The times are simulated.
256 devices in a mesh: layer: 4 (over x), row: 8 (over y, core), col: 8 (over z).
Axes of the slice: x: 4, y: 4, z: 8, core: 2. Of those that a mesh axis runs over, the one named last changes fastest.
Arguments:
- left_values: bfloat16 [8192, 4, 2048], P('row', 'layer', 'col'), may hold values from -22 to 22
- left_pattern: int32 [32, 4, 8], P('row', 'layer', 'col'), may hold values from 0 to 1, as said below
- right_values: bfloat16 [8192, 4, 2048], P(('layer', 'row'), None, 'col'), may hold values from -6 to 6
- right_pattern: int32 [32, 4, 8], P(('layer', 'row'), None, 'col'), may hold values from 0 to 1, as said below
Outputs:
- expanded: bfloat16 [8192, 4, 2048], P('row', 'layer', 'col')
Inputs may be any that keep to these rules, and one draw needn't show every extreme that they name: `left_pattern`: 1 marks a stored tile, 0 an absent one. `right_pattern`: 1 marks a stored tile, 0 an absent one.
All inputs are finite; a program needn't handle non-finite values.
Results may differ from a plain program's by a relative error of at most 0.001.
Values may be sent and summed in bfloat16 or wider, within the bound.
A program may use at most 64 MiB of HBM per device.

v0:
```python
import jax
import jax.numpy as jnp
from jax import lax
from jax.sharding import PartitionSpec as P


def expand_tiles(values, pattern):
    tile_rows, layers, tile_cols = pattern.shape
    tile_size = values.shape[0] // tile_rows
    blocks = values.reshape(tile_rows, tile_size, layers, tile_cols, tile_size)
    blocks = blocks * pattern[:, None, :, :, None].astype(values.dtype)
    return blocks.reshape(values.shape)


def per_device(left_values, left_pattern, right_values, right_pattern):
    left_block = expand_tiles(left_values, left_pattern)
    right_block = expand_tiles(right_values, right_pattern)
    rows_local = left_block.shape[0]
    columns_local = left_block.shape[2]
    left_flat = left_block.reshape(rows_local, columns_local)
    right_flat = right_block.reshape(right_block.shape[0], -1)
    right_all = lax.all_gather(right_flat, "row", axis=0, tiled=True)
    left_all = lax.all_gather(left_flat, "col", axis=1, tiled=True)
    partial = jnp.dot(left_all, right_all, preferred_element_type=jnp.float32)
    layers = lax.axis_size("layer")
    partial = jnp.stack(
        [partial[:, columns_local * l : columns_local * (l + 1)] for l in range(layers)], axis=0
    )
    product = lax.psum_scatter(partial, "layer", scatter_dimension=0, tiled=True)
    product = product.reshape(rows_local, 1, columns_local)
    squared = product * product
    column = lax.psum(jnp.sum(squared, axis=0, keepdims=True), "row")
    rows_total = rows_local * lax.axis_size("row")
    colmean = column / rows_total
    return (squared / (colmean + 1e-06)).astype(jnp.bfloat16)


def solution(mesh):
    return jax.shard_map(
        per_device,
        mesh=mesh,
        in_specs=(
            P("row", "layer", "col"),
            P("row", "layer", "col"),
            P(("layer", "row"), None, "col"),
            P(("layer", "row"), None, "col"),
        ),
        out_specs=P("row", "layer", "col"),
        check_vma=False,
    )
```

profile of v0, /device:TPU:32, one launch (start us, length us, event | category | flops | bytes accessed | tf_op | source)
XLA Modules:
  0.0 194.0 jit_solution(14705510479955236059)
XLA Ops:
  6.5 0.0 all-gather.3.cloned.1.call-start
  6.5 0.7 convert_bitcast_fusion.1
  7.2 0.1 broadcast_bitcast_fusion
  7.3 2.0 %bitcast_multiply_fusion = bf16[1024,256]{1,0:T(8,128)(2,1)} fusion(bf16[1024,1,256]{2,0,1:T(8,128)(2,1)} %param.4, bf16[1024]{0:T(1024)(128)(2,1)S(1)} %bitcast.29), kind=kLoop, calls=%fused_computation.8 | loop fusion | flops 262144 | bytes 1050624 | tf_op jit(solution)/shard_map/mul | solution.py:11
  9.3 0.0 all-gather.3.cloned.1.call-update
  9.3 0.0 all-gather.5.cloned.1.call-start
  9.4 0.7 convert_bitcast_fusion
  10.1 1.3 broadcast_multiply_fusion
  11.4 0.9 copy.6
  12.3 0.0 all-gather.5.cloned.1.call-update
  12.4 0.0 reduce-scatter.2.cloned.1.call-start
  12.4 62.3 %all-gather.3.cloned.1.call-done = bf16[1024,2048]{1,0:T(8,128)(2,1)} async-done(((bf16[1024,256]{1,0:T(8,128)(2,1)}), bf16[1024,2048]{1,0:T(8,128)(2,1)}) %all-gather.3.cloned.1.call-update) | async-done | bytes 4194320 | tf_op jit(solution)/shard_map/all_gather | solution.py:23
  74.7 35.0 %all-gather.5.cloned.1.call-done = bf16[2048,1024]{1,0:T(8,128)(2,1)} async-done(((bf16[256,1024]{1,0:T(8,128)(2,1)}), bf16[2048,1024]{1,0:T(8,128)(2,1)}) %all-gather.5.cloned.1.call-update) | async-done | bytes 4194320 | tf_op jit(solution)/shard_map/all_gather | solution.py:22
  109.7 7.5 %fusion.1 = f32[1024,1024]{1,0:T(8,128)S(1)} fusion(bf16[1024,2048]{1,0:T(8,128)(2,1)} %all-gather.3.cloned.1.call-done, bf16[2048,1024]{1,0:T(8,128)(2,1)} %all-gather.5.cloned.1.call-done), kind=kOutput, calls=%fused_computation.14 | convolution fusion | flops 4294967296 | bytes 12582912 | tf_op jit(solution)/shard_map/dot_general | solution.py:24
  117.2 0.4 slice_bitcast_fusion.3
  117.6 2.2 %pad_maximum_fusion = f32[4,1024,256]{2,1,0:T(8,128)} fusion(f32[1,1024,256]{2,1,0:T(8,128)S(1)} %get-tuple-element.6, f32[1,1024,256]{2,1,0:T(8,128)S(1)} %get-tuple-element.7, f32[1,1024,256]{2,1,0:T(8,128)S(1)} %get-tuple-element.8, f32[1,1024,256]{2,1,0:T(8,128)S(1)} %get-tuple-element.5), kind=kLoop, calls=%fused_computation | loop fusion | flops 3145728 | bytes 8388608 | tf_op jit(solution)/shard_map/stack | solution.py:26
  119.8 0.0 reduce-scatter.2.cloned.1.call-update
  119.8 49.5 %reduce-scatter.2.cloned.1.call-done = f32[1,1024,256]{2,1,0:T(8,128)} async-done(((f32[4,1024,256]{2,1,0:T(8,128)}), f32[1,1024,256]{2,1,0:T(8,128)}) %reduce-scatter.2.cloned.1.call-update) | async-done | bytes 1048592 | tf_op jit(solution)/shard_map/reduce_scatter | solution.py:29
  169.3 1.4 multiply_reduce_fusion
  170.7 14.6 %psum.7 = f32[1,1,256]{2,1,0:T(1,128)S(1)} all-reduce(f32[1,1,256]{2,1,0:T(1,128)S(1)} %bitcast.30), channel_id=1, replica_groups=mesh['layer'=4,'row'=8,'col'=8] {'row'}, use_global_device_ids=true, to_apply=%region_2.0 | all-reduce | flops 256 | bytes 2048 | tf_op jit(solution)/shard_map/psum | solution.py:32
  185.3 2.1 %fusion = bf16[1024,1,256]{2,0,1:T(8,128)(2,1)} fusion(f32[1,1024,256]{2,1,0:T(8,128)} %reduce-scatter.2.cloned.1.call-done, f32[256]{0:T(256)S(1)} %bitcast.31), kind=kLoop, calls=%fused_computation.6 | loop fusion | flops 786432 | bytes 1573888 | tf_op jit(solution)/shard_map/convert_element_type | solution.py:35
  (2 shorter events, 0.0 us)
Async XLA Ops:
  6.5 68.1 %all-gather.3.cloned.1.call-start = ((), (), s32[]{:S(2)}) async-start(), calls=%async_computation.1 | async-start | bytes 4718592 | tf_op jit(solution)/shard_map/all_gather | solution.py:23
  9.3 100.4 %all-gather.5.cloned.1.call-start = ((), (), s32[]{:S(2)}) async-start(), calls=%async_computation.2 | async-start | bytes 4718592 | tf_op jit(solution)/shard_map/all_gather | solution.py:22
  12.4 156.9 %reduce-scatter.2.cloned.1.call-start = ((), (), s32[]{:S(2)}) async-start(), calls=%async_computation.3 | async-start | bytes 5242880 | tf_op jit(solution)/shard_map/reduce_scatter | solution.py:29
Sparse Core Ops, SparseCore 0:
  9.5 65.1 all-gather.2
  76.5 33.1 all-gather.4
  120.0 49.2 reduce-scatter.1
where the time goes:
time: 194 us
  waiting for transfers between devices  147 us (76%)
  blocking collectives  14.6 us (8%)
  between operations  13.1 us (7%)
  other arithmetic  10.4 us (5%)
  matrix products  7.5 us (4%)
    all_gather x1, waiting for transfers between devices, per_device(): left_all = lax.all_gather(left_flat, 'col', axis=1, tiled=True)  62.3 us
    reduce_scatter x1, waiting for transfers between devices, per_device(): lax.psum_scatter(partial, 'layer', scatter_dimension=0, tiled=True)  49.5 us
    all_gather x1, waiting for transfers between devices, per_device(): right_all = lax.all_gather(right_flat, 'row', axis=0, tiled=True)  35 us
    psum x1, blocking collectives, per_device(): column = lax.psum(jnp.sum(squared, axis=0, keepdims=True), 'row')  14.6 us
    dot_general x1, matrix products, per_device(): partial = jnp.dot(left_all, right_all, preferred_element_type=jnp.float32)  7.5 us
  transfers between devices with their start and end apart: 3, of which 3 were waited for; matrix products, arithmetic and copies ran while one was open for 2% of the time, Pallas kernels for 0%

commit v1 on v0

--- a/solution.py
+++ b/solution.py
@@ -19,7 +19,12 @@
     columns_local = left_block.shape[2]
     left_flat = left_block.reshape(rows_local, columns_local)
     right_flat = right_block.reshape(right_block.shape[0], -1)
-    right_all = lax.all_gather(right_flat, "row", axis=0, tiled=True)
+    ring = [right_flat]
+    for hop in range(7):
+        ring.append(lax.ppermute(ring[-1], "row", [(dev, (dev + 1) % 8) for dev in range(8)]))
+    right_all = jnp.roll(
+        jnp.concatenate(ring[::-1], axis=0), (lax.axis_index("row") + 1) * ring[0].shape[0], axis=0
+    )
     left_all = lax.all_gather(left_flat, "col", axis=1, tiled=True)
     partial = jnp.dot(left_all, right_all, preferred_element_type=jnp.float32)
     layers = lax.axis_size("layer")

time: 194 us -> 183 us (0.943)
  waiting for transfers between devices: 147 us -> 119 us
  local copies, waits for them, and re-layouts: 1.42 us -> 18.1 us
    ppermute x0 -> x7, waiting for transfers between devices: none -> 69.1 us  [per_device(): lax.ppermute(ring[-1], 'row', [(dev, (dev + 1) % 8) for dev in range(8)])]
    all_gather x1, waiting for transfers between devices: 62.3 us -> 0.01 us  [per_device(): left_all = lax.all_gather(left_flat, 'col', axis=1, tiled=True)]
    all_gather x1 -> x0, waiting for transfers between devices: 35 us -> none  [per_device(): right_all = lax.all_gather(right_flat, 'row', axis=0, tiled=True)]
    unnamed x3 -> x18, local copies, waits for them, and re-layouts: 1.03 us -> 16.8 us
  transfers between devices with their start and end apart: 3 -> 9, of which waited for: 3 -> 8; matrix products, arithmetic and copies ran while one was open for 2% -> 11% of each run, Pallas kernels for 0% -> 0%
where the time goes in v1:
time: 183 us
  waiting for transfers between devices  119 us (65%)
  local copies, waits for them, and re-layouts  18.1 us (10%)
  blocking collectives  14.6 us (8%)
  between operations  13.5 us (7%)
  other arithmetic  10.4 us (6%)
  matrix products  7.51 us (4%)
    ppermute x7, waiting for transfers between devices, per_device(): lax.ppermute(ring[-1], 'row', [(dev, (dev + 1) % 8) for dev in range(8)])  69.1 us
    reduce_scatter x1, waiting for transfers between devices, per_device(): lax.psum_scatter(partial, 'layer', scatter_dimension=0, tiled=True)  49.5 us
    unnamed x18, local copies, waits for them, and re-layouts  16.8 us
    psum x1, blocking collectives, per_device(): column = lax.psum(jnp.sum(squared, axis=0, keepdims=True), 'row')  14.6 us
    dot_general x1, matrix products, per_device(): partial = jnp.dot(left_all, right_all, preferred_element_type=jnp.float32)  7.51 us
  transfers between devices with their start and end apart: 9, of which 8 were waited for; matrix products, arithmetic and copies ran while one was open for 11% of the time, Pallas kernels for 0%

profile of v1, /device:TPU:32, one launch (start us, length us, event | category | flops | bytes accessed | tf_op | source)
XLA Modules:
  0.0 182.7 jit_solution(17738077982640674386)
XLA Ops:
  7.3 2.0 %bitcast_multiply_fusion = bf16[1024,256]{1,0:T(8,128)(2,1)} fusion(bf16[1024,1,256]{2,0,1:T(8,128)(2,1)} %param.4, bf16[1024]{0:T(1024)(128)(2,1)S(1)} %bitcast.30), kind=kLoop, calls=%fused_computation.10 | loop fusion | flops 262144 | bytes 1050624 | tf_op jit(solution)/shard_map/mul | solution.py:11
  9.4 0.7 convert_bitcast_fusion
  10.1 1.3 broadcast_multiply_fusion
  11.5 9.8 %collective-permute-done = bf16[256,1024]{1,0:T(8,128)(2,1)S(1)} collective-permute-done((bf16[256,1024]{1,0:T(8,128)(2,1)S(1)}, bf16[256,1024]{1,0:T(8,128)(2,1)S(1)}, u32[]{:S(2)}, u32[]{:S(2)}) %collective-permute-start) | collective-permute-done | bytes 524320 | tf_op jit(solution)/shard_map/ppermute | solution.py:24
  21.3 9.8 %collective-permute-done.1 = bf16[256,1024]{1,0:T(8,128)(2,1)S(1)} collective-permute-done((bf16[256,1024]{1,0:T(8,128)(2,1)S(1)}, bf16[256,1024]{1,0:T(8,128)(2,1)S(1)}, u32[]{:S(2)}, u32[]{:S(2)}) %collective-permute-start.1) | collective-permute-done | bytes 524320 | tf_op jit(solution)/shard_map/ppermute | solution.py:24
  31.1 9.8 %collective-permute-done.2 = bf16[256,1024]{1,0:T(8,128)(2,1)S(1)} collective-permute-done((bf16[256,1024]{1,0:T(8,128)(2,1)S(1)}, bf16[256,1024]{1,0:T(8,128)(2,1)S(1)}, u32[]{:S(2)}, u32[]{:S(2)}) %collective-permute-start.2) | collective-permute-done | bytes 524320 | tf_op jit(solution)/shard_map/ppermute | solution.py:24
  41.0 9.8 %collective-permute-done.3 = bf16[256,1024]{1,0:T(8,128)(2,1)S(1)} collective-permute-done((bf16[256,1024]{1,0:T(8,128)(2,1)S(1)}, bf16[256,1024]{1,0:T(8,128)(2,1)S(1)}, u32[]{:S(2)}, u32[]{:S(2)}) %collective-permute-start.3) | collective-permute-done | bytes 524320 | tf_op jit(solution)/shard_map/ppermute | solution.py:24
  50.8 9.8 %collective-permute-done.4 = bf16[256,1024]{1,0:T(8,128)(2,1)S(1)} collective-permute-done((bf16[256,1024]{1,0:T(8,128)(2,1)S(1)}, bf16[256,1024]{1,0:T(8,128)(2,1)S(1)}, u32[]{:S(2)}, u32[]{:S(2)}) %collective-permute-start.4) | collective-permute-done | bytes 524320 | tf_op jit(solution)/shard_map/ppermute | solution.py:24
  60.6 9.9 %collective-permute-done.5 = bf16[256,1024]{1,0:T(8,128)(2,1)} collective-permute-done((bf16[256,1024]{1,0:T(8,128)(2,1)S(1)}, bf16[256,1024]{1,0:T(8,128)(2,1)}, u32[]{:S(2)}, u32[]{:S(2)}) %collective-permute-start.5) | collective-permute-done | bytes 524320 | tf_op jit(solution)/shard_map/ppermute | solution.py:24
  70.5 10.1 %collective-permute-done.6 = bf16[256,1024]{1,0:T(8,128)(2,1)} collective-permute-done((bf16[256,1024]{1,0:T(8,128)(2,1)}, bf16[256,1024]{1,0:T(8,128)(2,1)}, u32[]{:S(2)}, u32[]{:S(2)}) %collective-permute-start.6) | collective-permute-done | bytes 524320 | tf_op jit(solution)/shard_map/ppermute | solution.py:24
  80.6 1.9 %constant_dynamic-update-slice_fusion.15 = bf16[4096,1024]{1,0:T(8,128)(2,1)} fusion(bf16[256,1024]{1,0:T(8,128)(2,1)} %collective-permute-done.6), kind=kLoop, calls=%fused_computation.27 | loop fusion | bytes 1048576
  82.5 1.9 %constant_dynamic-update-slice_fusion.14 = bf16[4096,1024]{1,0:T(8,128)(2,1)} fusion(bf16[4096,1024]{1,0:T(8,128)(2,1)} %constant_dynamic-update-slice_fusion.15, bf16[256,1024]{1,0:T(8,128)(2,1)} %collective-permute-done.5), kind=kLoop, calls=%fused_computation.26 | loop fusion | bytes 1048576
  84.4 0.8 constant_dynamic-update-slice_fusion.13
  85.2 0.8 constant_dynamic-update-slice_fusion.12
  86.0 0.8 constant_dynamic-update-slice_fusion.11
  86.9 0.8 constant_dynamic-update-slice_fusion.10
  87.7 0.8 constant_dynamic-update-slice_fusion.9
  88.5 0.8 constant_dynamic-update-slice_fusion.8
  89.4 1.9 %constant_dynamic-update-slice_fusion.7 = bf16[4096,1024]{1,0:T(8,128)(2,1)} fusion(bf16[4096,1024]{1,0:T(8,128)(2,1)} %constant_dynamic-update-slice_fusion.8, bf16[256,1024]{1,0:T(8,128)(2,1)} %collective-permute-done.6), kind=kLoop, calls=%fused_computation.19 | loop fusion | bytes 1048576
  91.2 1.9 %constant_dynamic-update-slice_fusion.6 = bf16[4096,1024]{1,0:T(8,128)(2,1)} fusion(bf16[4096,1024]{1,0:T(8,128)(2,1)} %constant_dynamic-update-slice_fusion.7, bf16[256,1024]{1,0:T(8,128)(2,1)} %collective-permute-done.5), kind=kLoop, calls=%fused_computation.18 | loop fusion | bytes 1048576
  93.1 0.8 constant_dynamic-update-slice_fusion.5
  94.0 0.8 constant_dynamic-update-slice_fusion.4
  94.8 0.8 constant_dynamic-update-slice_fusion.3
  95.6 0.8 constant_dynamic-update-slice_fusion.2
  96.5 0.8 constant_dynamic-update-slice_fusion.1
  97.3 0.9 constant_dynamic-update-slice_fusion
  98.1 7.5 %fusion = f32[1024,1024]{1,0:T(8,128)S(1)} fusion(bf16[1024,2048]{1,0:T(8,128)(2,1)} %all-gather.2.cloned.1.call-done, bf16[4096,1024]{1,0:T(8,128)(2,1)} %constant_dynamic-update-slice_fusion, s32[]{:T(128)S(6)} %select_n.14), kind=kOutput, calls=%fused_computation.1 | convolution fusion | flops 4294967296 | bytes 12582916 | tf_op jit(solution)/shard_map/dot_general | solution.py:29
  106.1 2.2 %pad_maximum_fusion = f32[4,1024,256]{2,1,0:T(8,128)} fusion(f32[1,1024,256]{2,1,0:T(8,128)S(1)} %get-tuple-element.6, f32[1,1024,256]{2,1,0:T(8,128)S(1)} %get-tuple-element.7, f32[1,1024,256]{2,1,0:T(8,128)S(1)} %get-tuple-element.8, f32[1,1024,256]{2,1,0:T(8,128)S(1)} %get-tuple-element.5), kind=kLoop, calls=%fused_computation | loop fusion | flops 3145728 | bytes 8388608 | tf_op jit(solution)/shard_map/stack | solution.py:31
  108.3 49.5 %reduce-scatter.2.cloned.1.call-done = f32[1,1024,256]{2,1,0:T(8,128)} async-done(((f32[4,1024,256]{2,1,0:T(8,128)}), f32[1,1024,256]{2,1,0:T(8,128)}) %reduce-scatter.2.cloned.1.call-update) | async-done | bytes 1048592 | tf_op jit(solution)/shard_map/reduce_scatter | solution.py:34
  157.7 1.4 multiply_reduce_fusion
  159.1 14.6 %psum.7 = f32[1,1,256]{2,1,0:T(1,128)S(1)} all-reduce(f32[1,1,256]{2,1,0:T(1,128)S(1)} %bitcast.31), channel_id=1, replica_groups=mesh['layer'=4,'row'=8,'col'=8] {'row'}, use_global_device_ids=true, to_apply=%region_2.3 | all-reduce | flops 256 | bytes 2048 | tf_op jit(solution)/shard_map/psum | solution.py:37
  173.8 2.1 %fusion.2 = bf16[1024,1,256]{2,0,1:T(8,128)(2,1)} fusion(f32[1,1024,256]{2,1,0:T(8,128)} %reduce-scatter.2.cloned.1.call-done, f32[256]{0:T(256)S(1)} %bitcast.32), kind=kLoop, calls=%fused_computation.8 | loop fusion | flops 786432 | bytes 1573888 | tf_op jit(solution)/shard_map/convert_element_type | solution.py:40
  (18 shorter events, 1.3 us)
Async XLA Ops:
  6.5 91.6 %all-gather.2.cloned.1.call-start = ((), (), s32[]{:S(2)}) async-start(), calls=%async_computation.1 | async-start | bytes 4718592 | tf_op jit(solution)/shard_map/all_gather | solution.py:28
  9.3 148.4 %reduce-scatter.2.cloned.1.call-start = ((), (), s32[]{:S(2)}) async-start(), calls=%async_computation.2 | async-start | bytes 5242880 | tf_op jit(solution)/shard_map/reduce_scatter | solution.py:34
  11.5 9.8 %collective-permute-start = (bf16[256,1024]{1,0:T(8,128)(2,1)S(1)}, bf16[256,1024]{1,0:T(8,128)(2,1)S(1)}, u32[]{:S(2)}, u32[]{:S(2)}) collective-permute-start(bf16[256,1024]{1,0:T(8,128)(2,1)S(1)} %bitcast.26), channel_id=1, source_target_pairs={{0,8},{8,16},{16,24},{24,32},{32,40},{40,48},{48,56},{56,0},{1,9},... | collective-permute-start | bytes 1572872 | tf_op jit(solution)/shard_map/ppermute | solution.py:24
  21.3 9.8 %collective-permute-start.1 = (bf16[256,1024]{1,0:T(8,128)(2,1)S(1)}, bf16[256,1024]{1,0:T(8,128)(2,1)S(1)}, u32[]{:S(2)}, u32[]{:S(2)}) collective-permute-start(bf16[256,1024]{1,0:T(8,128)(2,1)S(1)} %collective-permute-done), channel_id=1, source_target_pairs={{0,8},{8,16},{16,24},{24,32},{32,40},{40,48},{48,56},{56,0},{1,9},... | collective-permute-start | bytes 1572872 | tf_op jit(solution)/shard_map/ppermute | solution.py:24
  31.1 9.8 %collective-permute-start.2 = (bf16[256,1024]{1,0:T(8,128)(2,1)S(1)}, bf16[256,1024]{1,0:T(8,128)(2,1)S(1)}, u32[]{:S(2)}, u32[]{:S(2)}) collective-permute-start(bf16[256,1024]{1,0:T(8,128)(2,1)S(1)} %collective-permute-done.1), channel_id=1, source_target_pairs={{0,8},{8,16},{16,24},{24,32},{32,40},{40,48},{48,56},{56,0},{1,9},... | collective-permute-start | bytes 1572872 | tf_op jit(solution)/shard_map/ppermute | solution.py:24
  41.0 9.8 %collective-permute-start.3 = (bf16[256,1024]{1,0:T(8,128)(2,1)S(1)}, bf16[256,1024]{1,0:T(8,128)(2,1)S(1)}, u32[]{:S(2)}, u32[]{:S(2)}) collective-permute-start(bf16[256,1024]{1,0:T(8,128)(2,1)S(1)} %collective-permute-done.2), channel_id=1, source_target_pairs={{0,8},{8,16},{16,24},{24,32},{32,40},{40,48},{48,56},{56,0},{1,9},... | collective-permute-start | bytes 1572872 | tf_op jit(solution)/shard_map/ppermute | solution.py:24
  50.8 9.8 %collective-permute-start.4 = (bf16[256,1024]{1,0:T(8,128)(2,1)S(1)}, bf16[256,1024]{1,0:T(8,128)(2,1)S(1)}, u32[]{:S(2)}, u32[]{:S(2)}) collective-permute-start(bf16[256,1024]{1,0:T(8,128)(2,1)S(1)} %collective-permute-done.3), channel_id=1, source_target_pairs={{0,8},{8,16},{16,24},{24,32},{32,40},{40,48},{48,56},{56,0},{1,9},... | collective-permute-start | bytes 1572872 | tf_op jit(solution)/shard_map/ppermute | solution.py:24
  60.6 9.9 %collective-permute-start.5 = (bf16[256,1024]{1,0:T(8,128)(2,1)S(1)}, bf16[256,1024]{1,0:T(8,128)(2,1)}, u32[]{:S(2)}, u32[]{:S(2)}) collective-permute-start(bf16[256,1024]{1,0:T(8,128)(2,1)S(1)} %collective-permute-done.4), channel_id=1, source_target_pairs={{0,8},{8,16},{16,24},{24,32},{32,40},{40,48},{48,56},{56,0},{1,9},... | collective-permute-start | bytes 1572872 | tf_op jit(solution)/shard_map/ppermute | solution.py:24
  70.5 10.1 %collective-permute-start.6 = (bf16[256,1024]{1,0:T(8,128)(2,1)}, bf16[256,1024]{1,0:T(8,128)(2,1)}, u32[]{:S(2)}, u32[]{:S(2)}) collective-permute-start(bf16[256,1024]{1,0:T(8,128)(2,1)} %collective-permute-done.5), channel_id=1, source_target_pairs={{0,8},{8,16},{16,24},{24,32},{32,40},{40,48},{48,56},{56,0},{1,9},... | collective-permute-start | bytes 1572872 | tf_op jit(solution)/shard_map/ppermute | solution.py:24
Sparse Core Ops, SparseCore 0:
  9.5 64.9 all-gather.1
  108.4 49.2 reduce-scatter.1
